TPU v7x, 32 devices: a whole 2x2x4 slice. The times are simulated.
32 devices in a mesh: dp: 16 (over z, y, x), mp: 2 (over core).
Axes of the slice: x: 2, y: 2, z: 4, core: 2. Of those that a mesh axis runs over, the one named last changes fastest.
Arguments:
- tokens: bfloat16 [16, 512, 768], P('dp'), may hold values from -6 to 6
- cotangent: float32 [16, 128, 768], P('dp'), may hold values from -6 to 6
- masked_pos: int32 [16, 128], P('dp'), may hold values from -1 to 511, as said below
- w_qkv: bfloat16 [3, 768, 768], P(None, None, 'mp'), may hold values from -0.21875 to 0.21875
- b_qkv: float32 [3, 768], P(None, 'mp'), may hold values from -3 to 3
- w_out: bfloat16 [768, 768], P('mp'), may hold values from -0.625 to 0.625
- b_out: float32 [768], replicated, may hold values from -3 to 3
- w_in: bfloat16 [768, 3072], P(None, 'mp'), may hold values from -0.21875 to 0.21875
- b_in: float32 [3072], P('mp'), may hold values from -3 to 3
- w_back: bfloat16 [3072, 768], P('mp'), may hold values from -0.109375 to 0.109375
- b_back: float32 [768], replicated, may hold values from -3 to 3
- ln_gain: float32 [2, 768], replicated, may hold values from 0.5 to 1.5
- ln_bias: float32 [2, 768], replicated, may hold values from -2 to 2
Outputs:
- output: bfloat16 [16, 512, 768], P('dp')
- grad_tokens: float32 [16, 512, 768], P('dp')
- grad_w_qkv: float32 [3, 768, 768], P(None, 'dp', 'mp')
- grad_b_qkv: float32 [3, 768], P(None, 'mp')
- grad_w_out: float32 [768, 768], P('mp', 'dp')
- grad_b_out: float32 [768], replicated
- grad_w_in: float32 [768, 3072], P('dp', 'mp')
- grad_b_in: float32 [3072], P('mp')
- grad_w_back: float32 [3072, 768], P('mp', 'dp')
- grad_b_back: float32 [768], replicated
- grad_ln_gain: float32 [2, 768], replicated
- grad_ln_bias: float32 [2, 768], replicated
Inputs may be any that keep to these rules, and one draw needn't show every extreme that they name: `masked_pos`: each row lists between 25 and 128 distinct positions in increasing order, then -1 in the remaining slots; some row lists exactly 128.
All inputs are finite; a program needn't handle non-finite values.
Results may differ from a plain program's by a relative error of at most 0.014.
Values sent between devices are 32-bit elements; how exact they have to be, the bound alone decides.
No kernel may reach another device: no remote copies, remote signals or barrier semaphores. Data moves between devices by JAX's collectives and lax.ppermute only.
A program may use at most 128 MiB of HBM per device.

v0:
```python
import jax
import jax.numpy as jnp
import numpy as np
from jax import lax
from jax.experimental import pallas as pl
from jax.experimental.pallas import tpu as pltpu
from jax.sharding import PartitionSpec as P


HEAD_DIM = 64
PAIR = 2 * HEAD_DIM
EPS = 1e-06
F32 = jnp.float32
LOW = jnp.bfloat16


def tables(length):
    half = HEAD_DIM // 2
    freq = np.float32(10000.0) ** (-np.arange(half).astype(np.float32) / np.float32(half))
    angle = np.arange(length).astype(np.float32)[:, None] * freq.astype(np.float32)
    cosine = np.cos(angle).astype(np.float32)
    sine = np.sin(angle).astype(np.float32)
    cos_pair = np.concatenate([cosine] * 4, 1)
    sin_pair = np.concatenate([-sine, sine, -sine, sine], 1)
    return jnp.asarray(cos_pair), jnp.asarray(sin_pair)


def dot(left, right):
    return jnp.dot(left, right, preferred_element_type=F32)


def dot_nt(left, right):
    return lax.dot_general(left, right, (((1,), (1,)), ((), ())), preferred_element_type=F32)


def dot_tn(left, right):
    return lax.dot_general(left, right, (((0,), (0,)), ((), ())), preferred_element_type=F32)


def first_half(shape):
    return lax.broadcasted_iota(jnp.int32, shape, 1) % HEAD_DIM < HEAD_DIM // 2


def first_head(shape):
    return lax.broadcasted_iota(jnp.int32, shape, 1) < HEAD_DIM


def swapped(value):
    half = HEAD_DIM // 2
    ahead = pltpu.roll(value, PAIR - half, 1)
    behind = pltpu.roll(value, half, 1)
    return jnp.where(first_half(value.shape), ahead, behind)


def turn(value, cosine, sine):
    return value * cosine + swapped(value) * sine


def center_of(value):
    center = value - jnp.mean(value, -1, keepdims=True)
    scale = lax.rsqrt(jnp.mean(center * center, -1, keepdims=True) + EPS)
    return center * scale, scale


def norm_back(grad, hat, scale, gain):
    grad_hat = grad * gain
    mean_one = jnp.mean(grad_hat, -1, keepdims=True)
    mean_two = jnp.mean(grad_hat * hat, -1, keepdims=True)
    return scale * (grad_hat - mean_one - hat * mean_two)


def cdf_of(value):
    return 0.5 * (1.0 + lax.erf(value * np.float32(0.5**0.5)))


def gelu_slope(value, cdf):
    return cdf + value * (np.float32(1 / (2 * np.pi) ** 0.5) * jnp.exp(-0.5 * value * value))


def one_hot(pos_ref, length):
    pos = pos_ref[...]
    return lax.broadcasted_iota(jnp.int32, (pos.shape[0], length), 1) == pos


def col_sum(value):
    return jnp.sum(value, 0, keepdims=True)


def softmax_of(scores):
    expo = jnp.exp(scores - jnp.max(scores, -1, keepdims=True))
    return expo / jnp.sum(expo, -1, keepdims=True)


def front_kernel(
    tok, w_qkv, b_qkv, cos, sin, pos, w_out, q_o, k_o, v_o, qs_o, ts_o, cs_o, ss_o, prob_o, ctx_o, attn_o
):
    length = tok.shape[0]
    local = w_qkv.shape[2]
    pairs = local // PAIR
    hot_f = one_hot(pos, length).astype(F32)
    hot = hot_f.astype(LOW)
    rows = tok[...]
    ts_o[...] = dot(hot, rows).astype(LOW)
    cs_o[...] = jnp.dot(hot_f, cos[...], precision=lax.Precision.HIGHEST)
    ss_o[...] = jnp.dot(hot_f, sin[...], precision=lax.Precision.HIGHEST)
    pre_q = dot(rows, w_qkv[0]) + b_qkv[0:1, :]
    pre_k = dot(rows, w_qkv[1]) + b_qkv[1:2, :]
    v_o[...] = (dot(rows, w_qkv[2]) + b_qkv[2:3, :]).astype(LOW)
    for j in range(pairs):
        cut = slice(j * PAIR, (j + 1) * PAIR)
        q_o[:, cut] = turn(pre_q[:, cut], cos[...], sin[...]).astype(LOW)
        k_o[:, cut] = turn(pre_k[:, cut], cos[...], sin[...]).astype(LOW)
    qs_o[...] = dot(hot, q_o[...]).astype(LOW)
    for j in range(pairs):
        cut = slice(j * PAIR, (j + 1) * PAIR)
        query = qs_o[:, cut]
        keys = k_o[:, cut]
        values = v_o[:, cut]
        lead = first_head(query.shape)
        parts = []
        for side in range(2):
            chosen = jnp.where(lead if side == 0 else ~lead, query.astype(F32), 0.0).astype(LOW)
            prob = softmax_of(dot_nt(chosen, keys) * HEAD_DIM**-0.5)
            prob_o[2 * j + side] = prob
            parts.append(dot(prob.astype(LOW), values))
        ctx_o[:, cut] = jnp.where(lead, parts[0], parts[1]).astype(LOW)
    attn_o[...] = dot(ctx_o[...], w_out[...])


def mid_kernel(
    mine, other, tok, b_out, gain, shift, w_in, b_in, w_back, one_o, part_o, hat_o, scale_o, slope_o
):
    h_pre = tok[...].astype(F32) + (mine[...] + other[...] + b_out[...])
    hat, scale = center_of(h_pre)
    h_one = hat * gain[0:1, :] + shift[0:1, :]
    one_o[...] = h_one
    hidden = dot(h_one.astype(LOW), w_in[...]) + b_in[...]
    cdf = cdf_of(hidden)
    part_o[...] = dot((hidden * cdf).astype(LOW), w_back[...])
    hat_o[...] = hat
    scale_o[...] = scale
    slope_o[...] = gelu_slope(hidden, cdf)


def turn_kernel(
    mpi, mine, other, h_one, b_back, gain, cot, pos, slope, w_in, w_back, gz_o, half_o, part_o, small_o
):
    width = h_one.shape[1]
    z_sum = h_one[...] + (mine[...] + other[...] + b_back[...])
    hat, scale = center_of(z_sum)
    grad = jnp.where(pos[...] >= 0, cot[...], 0.0)
    grad_z = norm_back(grad, hat, scale, gain[1:2, :])
    gz_o[...] = grad_z
    count = half_o.shape[0] // 2
    half_o[:count] = jnp.where(mpi[0] == 0, h_one[:count], h_one[count:])
    half_o[count:] = jnp.where(mpi[0] == 0, grad_z[:count], grad_z[count:])
    grad_y = grad_z.astype(LOW)
    grad_u = (dot_nt(grad_y, w_back[...]) * slope[...]).astype(LOW)
    part_o[...] = dot_nt(grad_u, w_in[...])
    small_o[...] = jnp.zeros(small_o.shape, F32)
    small_o[0:1, :] = col_sum(grad_u.astype(F32))
    small_o[2:3, width:] = col_sum(grad_y.astype(F32))
    small_o[3:4, width:] = col_sum(grad * hat)
    small_o[4:5, width:] = col_sum(grad)


def back_kernel(
    place, mine, other, grad_z, hat, scale, gain, tok, tok_sel, ctx, w_out, q_sel, keys, values, prob,
    cos, sin, cos_sel, sin_sel, small,
    a_keep, a_send, b_keep, b_send, gq_s, gk_s, gv_s, small_o, pre_o,
):
    _, width = tok.shape
    local = w_out.shape[0]
    pairs = local // PAIR
    near = a_keep.shape[0]
    blocks = 2 * near
    chunk = width // blocks
    grad_h = mine[...] + other[...] + grad_z[...]
    g_pre = norm_back(grad_h, hat[...], scale[...], gain[0:1, :])
    pre_o[...] = g_pre
    g_attn = g_pre.astype(LOW)
    small_o[...] = small[...]
    small_o[2:3, :width] = col_sum(g_attn.astype(F32))
    small_o[3:4, :width] = col_sum(grad_h * hat[...])
    small_o[4:5, :width] = col_sum(grad_h)

    def spread(keep, send, order, left, right):
        for c in range(blocks):
            rows_of = slice(c * chunk, (c + 1) * chunk)
            spot = place[order, c]

            @pl.when(spot < near)
            def _():
                keep[spot, :, :local] = left[rows_of]
                keep[spot, :, local:] = right[rows_of]

            @pl.when(spot >= near)
            def _():
                send[spot - near, :, :local] = left[rows_of]
                send[spot - near, :, local:] = right[rows_of]

    dw_out = dot_tn(g_attn, ctx[...])
    g_ctx = dot_nt(g_attn, w_out[...]).astype(LOW)
    for j in range(pairs):
        cut = slice(j * PAIR, (j + 1) * PAIR)
        key_pair = keys[:, cut]
        value_pair = values[:, cut]
        query_pair = q_sel[:, cut].astype(F32)
        ctx_pair = g_ctx[:, cut].astype(F32)
        lead = first_head(query_pair.shape)
        g_q, g_k, g_v = [], None, None
        for side in range(2):
            keep = lead if side == 0 else ~lead
            q_one = jnp.where(keep, query_pair, 0.0).astype(LOW)
            c_one = jnp.where(keep, ctx_pair, 0.0).astype(LOW)
            weight = prob[2 * j + side]
            g_prob = dot_nt(c_one, value_pair)
            inner = jnp.sum(weight * g_prob, -1, keepdims=True)
            g_score = (weight * (g_prob - inner)).astype(LOW)
            add_v = dot_tn(weight.astype(LOW), c_one)
            add_k = dot_tn(g_score, q_one)
            g_v = add_v if g_v is None else g_v + add_v
            g_k = add_k if g_k is None else g_k + add_k
            g_q.append(dot(g_score, key_pair))
        g_q = jnp.where(lead, g_q[0], g_q[1]) * HEAD_DIM**-0.5
        g_k = g_k * HEAD_DIM**-0.5
        gq_s[:, cut] = turn(g_q, cos_sel[...], -sin_sel[...]).astype(LOW)
        gk_s[:, cut] = turn(g_k, cos[...], -sin[...]).astype(LOW)
        gv_s[:, cut] = g_v.astype(LOW)
    rows = tok[...]
    spread(a_keep, a_send, 0, dw_out, dot_tn(tok_sel[...], gq_s[...]))
    spread(b_keep, b_send, 1, dot_tn(rows, gk_s[...]), dot_tn(rows, gv_s[...]))
    small_o[1:2, 0:local] = col_sum(gq_s[...].astype(F32))
    small_o[1:2, local : 2 * local] = col_sum(gk_s[...].astype(F32))
    small_o[1:2, 2 * local : 3 * local] = col_sum(gv_s[...].astype(F32))


def tokens_kernel(mpi, g_q, g_k, g_v, w_qkv, pos, g_pre, part_o):
    hot = one_hot(pos, g_k.shape[0]).astype(F32).astype(LOW)
    gq_full = dot_tn(hot, g_q[...]).astype(LOW)
    total = dot_nt(gq_full, w_qkv[0]) + dot_nt(g_k[...], w_qkv[1]) + dot_nt(g_v[...], w_qkv[2])
    part_o[...] = total

    @pl.when(mpi[0] == 0)
    def _():
        left = g_pre[...]
        spread = part_o[...]
        for _ in range(3):
            piece = left.astype(LOW)
            left = left - piece.astype(F32)
            spread = spread + dot_tn(hot, piece)
        part_o[...] = spread


def attend_kernel(query, keys, values, w_out, attn_o, ctx_s):
    pairs = query.shape[1] // PAIR
    for j in range(pairs):
        cut = slice(j * PAIR, (j + 1) * PAIR)
        q_pair = query[:, cut].astype(F32)
        lead = first_head(q_pair.shape)
        parts = []
        for side in range(2):
            chosen = jnp.where(lead if side == 0 else ~lead, q_pair, 0.0).astype(LOW)
            prob = softmax_of(dot_nt(chosen, keys[:, cut]) * HEAD_DIM**-0.5)
            parts.append(dot(prob.astype(LOW), values[:, cut]))
        ctx_s[:, cut] = jnp.where(lead, parts[0], parts[1]).astype(LOW)
    attn_o[...] = dot(ctx_s[...], w_out[...])


def feed_kernel(mine, other, tok, b_out, gain, shift, w_in, b_in, w_back, one_o, part_o):
    h_pre = tok[...].astype(F32) + (mine[...] + other[...] + b_out[...])
    hat, _ = center_of(h_pre)
    h_one = hat * gain[0:1, :] + shift[0:1, :]
    one_o[...] = h_one
    hidden = dot(h_one.astype(LOW), w_in[...]) + b_in[...]
    part_o[...] = dot((hidden * cdf_of(hidden)).astype(LOW), w_back[...])


def last_kernel(mine, other, h_one, b_back, gain, shift, out_o):
    z_sum = h_one[...] + (mine[...] + other[...] + b_back[...])
    hat, _ = center_of(z_sum)
    out_o[...] = (hat * gain[1:2, :] + shift[1:2, :]).astype(LOW)


def grads_kernel(
    h_one, grad_z, far_a, far_b, far_c, flipped, w_in, b_in, w_back, sel_in, sel_back,
    in_keep, in_send, back_keep, back_send,
):
    near, chunk = in_keep.shape[:2]
    part = far_a.shape[0] // 2
    fars = [far_a[...], far_b[...], far_c[...], flipped[...]]
    h_rows = [h_one[...]]
    g_rows = [grad_z[...]]
    for block in fars:
        for start in range(0, block.shape[0], 2 * part):
            h_rows.append(block[start : start + part])
            g_rows.append(block[start + part : start + 2 * part])
    h_low = jnp.concatenate(h_rows, 0).astype(LOW)
    g_low = jnp.concatenate(g_rows, 0).astype(LOW)
    hidden = dot(h_low, w_in[...]) + b_in[...]
    cdf = cdf_of(hidden)
    act = (hidden * cdf).astype(LOW)
    grad_u = (dot_nt(g_low, w_back[...]) * gelu_slope(hidden, cdf)).astype(LOW)
    h_cols = dot(h_low, sel_in[...]).astype(LOW)
    g_cols = dot(g_low, sel_back[...]).astype(LOW)
    d_in = dot_tn(h_cols, grad_u)
    d_back = dot_tn(g_cols, act)
    for c in range(near):
        in_keep[c] = d_in[c * chunk : (c + 1) * chunk]
        back_keep[c] = d_back[c * chunk : (c + 1) * chunk]
        in_send[c] = d_in[(near + c) * chunk : (near + c + 1) * chunk]
        back_send[c] = d_back[(near + c) * chunk : (near + c + 1) * chunk]


def finish_feed_kernel(keep_in, got_in, keep_back, got_back, in_o, back_o):
    in_o[...] = keep_in[0] + got_in[0]
    back_o[...] = keep_back[0] + got_back[0]


def finish_heads_kernel(keep_a, got_a, keep_b, got_b, out_o, qkv_o):
    local = out_o.shape[1]
    out_o[...] = keep_a[0, :, :local] + got_a[0, :, :local]
    qkv_o[0] = keep_a[0, :, local:] + got_a[0, :, local:]
    qkv_o[1] = keep_b[0, :, :local] + got_b[0, :, :local]
    qkv_o[2] = keep_b[0, :, local:] + got_b[0, :, local:]


def call(kernel, outs, *args, scalars=0, scratch=()):
    specs = [pl.BlockSpec(memory_space=pltpu.SMEM)] * scalars
    specs += [pl.BlockSpec(memory_space=pltpu.VMEM)] * (len(args) - scalars)
    shapes = [jax.ShapeDtypeStruct(*item) for item in outs]
    result = pl.pallas_call(
        kernel,
        out_shape=shapes if len(shapes) > 1 else shapes[0],
        in_specs=specs,
        scratch_shapes=list(scratch),
    )
    return result(*args)


def shards(
    count,
    tokens,
    cotangent,
    masked_pos,
    w_qkv,
    b_qkv,
    w_out,
    b_out,
    w_in,
    b_in,
    w_back,
    b_back,
    ln_gain,
    ln_bias,
):
    _, length, width = tokens.shape
    local = w_qkv.shape[2]
    hidden = w_in.shape[1]
    slots = masked_pos.shape[1]
    heads = local // HEAD_DIM
    bits = count.bit_length() - 1
    chunk = width // count
    near = count // 4
    near_bits = bits - 2
    me = lax.axis_index("dp")
    core = lax.axis_index("mp").astype(jnp.int32)[None]
    cos, sin = tables(length)

    def flip(value):
        return lax.ppermute(value, "mp", [(0, 1), (1, 0)])

    def across(value, bit):
        return lax.ppermute(value, "dp", [(i, i ^ (1 << bit)) for i in range(count)])

    def halve(keep, send, order):
        for bit in order:
            got = across(send, bit)
            half = got.shape[0] // 2
            if half:
                send = keep[half:] + got[half:]
                keep = keep[:half] + got[:half]
        return keep, got

    def slot_of(index, order):
        total = jnp.zeros_like(index)
        for at, bit in enumerate(order):
            total = total + (((index >> bit) & 1) << (len(order) - 1 - at))
        return total

    z_low, z_high = bits - 2, bits - 1
    rest = list(range(2, near_bits))
    order_a = [0, 1] + rest + [z_low, z_high]
    order_b = [1, z_low, 0] + rest + [z_high]
    order_in = [0, 1] + rest
    order_back = [1, 0] + rest
    delta = jnp.arange(count, dtype=jnp.int32) ^ me.astype(jnp.int32)
    place = jnp.stack([slot_of(delta, o) for o in (order_a, order_b)])

    def columns(order):
        index = jnp.arange(width, dtype=jnp.int32)
        number = index // chunk
        spot = slot_of((number % near) ^ (me % near).astype(jnp.int32), order) * chunk + index % chunk
        spot = jnp.where(number // near == me // near, spot, -1)
        return (spot[:, None] == jnp.arange(near * chunk, dtype=jnp.int32)).astype(LOW)

    sel_in = columns(order_in)
    sel_back = columns(order_back)

    def gather_far(value):
        return [
            lax.ppermute(value, "dp", [(i, (i + step * near) % count) for i in range(count)])
            for step in (2, 1, 3)
        ]

    tok = tokens[0]
    cot = cotangent[0]
    pos = masked_pos.reshape(slots, 1)
    b_out, b_in, b_back = b_out[None], b_in[None], b_back[None]

    query, keys, values, q_sel, tok_sel, cos_sel, sin_sel, prob, ctx_sel, attn = call(
        front_kernel,
        [
            ((length, local), LOW),
            ((length, local), LOW),
            ((length, local), LOW),
            ((slots, local), LOW),
            ((slots, width), LOW),
            ((slots, PAIR), F32),
            ((slots, PAIR), F32),
            ((heads, slots, length), F32),
            ((slots, local), LOW),
            ((slots, width), F32),
        ],
        tok, w_qkv, b_qkv, cos, sin, pos, w_out,
    )
    h_one, part, hat, scale, slope = call(
        mid_kernel,
        [
            ((slots, width), F32),
            ((slots, width), F32),
            ((slots, width), F32),
            ((slots, 1), F32),
            ((slots, hidden), F32),
        ],
        attn, flip(attn), tok_sel, b_out, ln_gain, ln_bias, w_in, b_in, w_back,
    )
    grad_z, half_rows, part, small = call(
        turn_kernel,
        [
            ((slots, width), F32),
            ((slots, width), F32),
            ((slots, width), F32),
            ((8, hidden), F32),
        ],
        core, part, flip(part), h_one, b_back, ln_gain, cot, pos, slope, w_in, w_back,
        scalars=1,
    )
    grad_h_other = flip(part)
    far = gather_far(half_rows)
    far_flipped = flip(jnp.concatenate(far, 0))
    shape = ((count // 2, chunk, 2 * local), F32)
    a_keep, a_send, b_keep, b_send, g_q, g_k, g_v, small, g_pre = call(
        back_kernel,
        [
            shape,
            shape,
            shape,
            shape,
            ((slots, local), LOW),
            ((length, local), LOW),
            ((length, local), LOW),
            ((8, hidden), F32),
            ((slots, width), F32),
        ],
        place, part, grad_h_other, grad_z, hat, scale, ln_gain, tok, tok_sel, ctx_sel, w_out, q_sel, keys, values,
        prob, cos, sin, cos_sel, sin_sel, small,
        scalars=1,
    )
    back_part = call(tokens_kernel, [((length, width), F32)], core, g_q, g_k, g_v, w_qkv, pos, g_pre, scalars=1)
    shape = ((near // 2, chunk, hidden), F32)
    in_keep, in_send, back_keep, back_send = call(
        grads_kernel, [shape] * 4, h_one, grad_z, *far, far_flipped, w_in, b_in, w_back, sel_in, sel_back
    )
    query, g_pre = lax.optimization_barrier((query, g_pre))
    attn = call(
        attend_kernel, [((length, width), F32)], query, keys, values, w_out,
        scratch=[pltpu.VMEM((length, local), LOW)],
    )
    h_full, part = call(
        feed_kernel,
        [((length, width), F32), ((length, width), F32)],
        attn, flip(attn), tok, b_out, ln_gain, ln_bias, w_in, b_in, w_back,
    )
    output = call(
        last_kernel, [((length, width), LOW)], part, flip(part), h_full, b_back, ln_gain, ln_bias
    )
    grad_tokens = jnp.add(back_part, flip(back_part))
    for bit in range(bits):
        small = small + across(small, bit)
    last_a = halve(a_keep, a_send, order_a)
    last_b = halve(b_keep, b_send, order_b)
    last_in = halve(in_keep, in_send, order_in)
    last_back = halve(back_keep, back_send, order_back)
    sum_in, sum_back = call(
        finish_feed_kernel, [((chunk, hidden), F32)] * 2, *last_in, *last_back
    )
    sum_out, sum_qkv = call(
        finish_heads_kernel, [((chunk, local), F32), ((3, chunk, local), F32)], *last_a, *last_b
    )
    return (
        output[None],
        grad_tokens[None],
        sum_qkv,
        small[1, : 3 * local].reshape(3, local),
        sum_out.T,
        small[2, :width],
        sum_in,
        small[0],
        sum_back.T,
        small[2, width:],
        small[3].reshape(2, width),
        small[4].reshape(2, width),
    )


def solution(mesh):
    in_specs = (
        P("dp", None, None),
        P("dp", None, None),
        P("dp", None),
        P(None, None, "mp"),
        P(None, "mp"),
        P("mp", None),
        P(),
        P(None, "mp"),
        P("mp"),
        P("mp", None),
        P(),
        P(),
        P(),
    )
    out_specs = (
        P("dp", None, None),
        P("dp", None, None),
        P(None, "dp", "mp"),
        P(None, "mp"),
        P("mp", "dp"),
        P(),
        P("dp", "mp"),
        P("mp"),
        P("mp", "dp"),
        P(),
        P(),
        P(),
    )
    count = mesh.shape["dp"]

    def body(*args):
        return shards(count, *args)

    return jax.shard_map(body, mesh=mesh, in_specs=in_specs, out_specs=out_specs, check_vma=False)
```

profile of v0, /device:TPU:0, one launch (start us, length us, event | category | flops | bytes accessed | tf_op | source)
XLA Modules:
  0.0 203.9 jit_solution(2409324461556060572)
XLA Ops:
  2.0 7.7 %shard_map.238 = (bf16[512,384]{1,0:T(8,128)(2,1)}, bf16[512,384]{1,0:T(8,128)(2,1)}, bf16[512,384]{1,0:T(8,128)(2,1)}, bf16[128,384]{1,0:T(8,128)(2,1)}, bf16[1...) custom-call(bf16[512,768]{1,0:T(8,128)(2,1)} %bitcast.9, ...), custom_call_target="tpu_custom_call" | custom-call | tf_op jit(solution)/shard_map/pallas_call | solution.py:338
  12.5 4.8 %shard_map.239 = (f32[128,768]{1,0:T(8,128)}, f32[128,768]{1,0:T(8,128)}, f32[128,768]{1,0:T(8,128)}, f32[128,1]{1,0:T(8,128)}, f32[128,1536]{1,0:T(8,128)}) custom-call(f32[128,768]{1,0:T(8,128)} %get-tuple-element.52.mine, f32[128,768]{1,0:T(8,128)} %copy-done.9, bf16[128,768]{1,0:T(8,128)(2,1)} %get-tuple-element.53.tok.tok_sel, ...), custom_call_target="tpu_custom_call" | custom-call | tf_op jit(solution)/shard_map/pallas_call | solution.py:338
  20.0 6.0 %shard_map.240 = (f32[128,768]{1,0:T(8,128)}, f32[128,768]{1,0:T(8,128)}, f32[128,768]{1,0:T(8,128)}, f32[8,1536]{1,0:T(8,128)}) custom-call(s32[1]{0:T(128)} %bitcast.2.mpi, f32[128,768]{1,0:T(8,128)} %get-tuple-element.54.mine, f32[128,768]{1,0:T(8,128)} %copy-done.8, f32[128,768]{1,0:T(8,128)} %get-tuple-element.55.h_one, ...), custom_call_target="tpu_custom_call" | custom-call | tf_op jit(solution)/shard_map/pallas_call | solution.py:338
  25.9 4.9 %collective-permute-start.20 = (f32[128,768]{1,0:T(8,128)}, f32[128,768]{1,0:T(8,128)S(1)}, u32[]{:S(2)}, u32[]{:S(2)}) collective-permute-start(f32[128,768]{1,0:T(8,128)} %get-tuple-element.83), channel_id=1, source_target_pairs={{0,24},{2,26},{4,28},{6,30},{8,0},{10,2},{12,4},{14,6},{16,8},{18,... | collective-permute-start | bytes 1179656 | tf_op jit(solution)/shard_map/ppermute | solution.py:412
  31.9 8.9 %collective-permute-done.20.far_c = f32[128,768]{1,0:T(8,128)S(1)} collective-permute-done((f32[128,768]{1,0:T(8,128)}, f32[128,768]{1,0:T(8,128)S(1)}, u32[]{:S(2)}, u32[]{:S(2)}) %collective-permute-start.20) | collective-permute-done | bytes 393248 | tf_op jit(solution)/shard_map/ppermute | solution.py:412
  40.8 9.3 %collective-permute-done.19.far_b = f32[128,768]{1,0:T(8,128)S(1)} collective-permute-done((f32[128,768]{1,0:T(8,128)}, f32[128,768]{1,0:T(8,128)S(1)}, u32[]{:S(2)}, u32[]{:S(2)}) %collective-permute-start.19) | collective-permute-done | bytes 393248 | tf_op jit(solution)/shard_map/ppermute | solution.py:412
  50.0 14.9 %collective-permute-done.18.far_a = f32[128,768]{1,0:T(8,128)S(1)} collective-permute-done((f32[128,768]{1,0:T(8,128)}, f32[128,768]{1,0:T(8,128)S(1)}, u32[]{:S(2)}, u32[]{:S(2)}) %collective-permute-start.18) | collective-permute-done | bytes 393248 | tf_op jit(solution)/shard_map/ppermute | solution.py:412
  67.5 10.6 %shard_map.241 = (f32[8,48,768]{2,1,0:T(8,128)}, f32[8,48,768]{2,1,0:T(8,128)}, f32[8,48,768]{2,1,0:T(8,128)}, f32[8,48,768]{2,1,0:T(8,128)}, bf16[128,384]{1,0:...) custom-call(s32[2,16]{1,0:T(2,128)} %pad_add_fusion.place, ...), custom_call_target="tpu_custom_call" | custom-call | tf_op jit(solution)/shard_map/pallas_call | solution.py:338
  79.7 5.7 %shard_map.242.mine = f32[512,768]{1,0:T(8,128)} custom-call(bf16[512,384]{1,0:T(8,128)(2,1)} %get-tuple-element.70.query, bf16[512,384]{1,0:T(8,128)(2,1)} %get-tuple-element.63.keys, bf16[512,384]{1,0:T(8,128)(2,1)} %get-tuple-element.64.values, bf16[384,768]{1,0:T(8,128)(2,1)} %w_out.5), custom_call_target="tpu_custom_call" | custom-call | tf_op jit(solution)/shard_map/pallas_call | solution.py:338
  87.6 20.2 %collective-permute-done.14 = f32[8,1536]{1,0:T(8,128)S(1)} collective-permute-done((f32[8,1536]{1,0:T(8,128)S(1)}, f32[8,1536]{1,0:T(8,128)S(1)}, u32[]{:S(2)}, u32[]{:S(2)}) %collective-permute-start.14) | collective-permute-done | bytes 49184 | tf_op jit(solution)/shard_map/ppermute | solution.py:374
  109.4 5.8 %collective-permute-done.15 = f32[8,1536]{1,0:T(8,128)S(1)} collective-permute-done((f32[8,1536]{1,0:T(8,128)S(1)}, f32[8,1536]{1,0:T(8,128)S(1)}, u32[]{:S(2)}, u32[]{:S(2)}) %collective-permute-start.15) | collective-permute-done | bytes 49184 | tf_op jit(solution)/shard_map/ppermute | solution.py:374
  116.2 3.2 %collective-permute-done.16 = f32[8,1536]{1,0:T(8,128)S(1)} collective-permute-done((f32[8,1536]{1,0:T(8,128)S(1)}, f32[8,1536]{1,0:T(8,128)S(1)}, u32[]{:S(2)}, u32[]{:S(2)}) %collective-permute-start.16) | collective-permute-done | bytes 49184 | tf_op jit(solution)/shard_map/ppermute | solution.py:374
  121.6 5.4 %shard_map.245 = f32[512,768]{1,0:T(8,128)} custom-call(s32[1]{0:T(128)} %bitcast.2.mpi, bf16[128,384]{1,0:T(8,128)(2,1)} %get-tuple-element.73.g_q, bf16[512,384]{1,0:T(8,128)(2,1)} %get-tuple-element.74.g_k, bf16[512,384]{1,0:T(8,128)(2,1)} %get-tuple-element.75.g_v, bf16[3,768,384]{2,1,0:T(8,128)(2,1)} %w_qkv.3, s32[128,1]{1,0:T(8,128)} %copy.27.pos, ...), custom_call_target="tpu_custom_call" | custom-call | tf_op jit(solution)/shard_map/pallas_call | solution.py:338
  129.3 8.7 %shard_map.247 = (f32[2,48,1536]{2,1,0:T(8,128)}, f32[2,48,1536]{2,1,0:T(8,128)}, f32[2,48,1536]{2,1,0:T(8,128)}, f32[2,48,1536]{2,1,0:T(8,128)}) custom-call(f32[128,768]{1,0:T(8,128)} %get-tuple-element.55.h_one, f32[128,768]{1,0:T(8,128)} %get-tuple-element.58.grad_z, f32[128,768]{1,0:T(8,128)} %copy-done.3, f32[128,768]{1,0:T(8,128)} %copy-done.2, ...), custom_call_target="tpu_custom_call" | custom-call | tf_op jit(solution)/shard_map/pallas_call | solution.py:338
  142.9 2.6 %slice_add_fusion.3 = (f32[4,48,768]{2,1,0:T(8,128)S(1)}, f32[4,48,768]{2,1,0:T(8,128)}) fusion(f32[8,48,768]{2,1,0:T(8,128)} %collective-permute-done.6, f32[8,48,768]{2,1,0:T(8,128)} %get-tuple-element.76), kind=kLoop, calls=%fused_computation.9 | loop fusion | flops 294912 | bytes 3538944 | tf_op jit(solution)/shard_map/add | solution.py:382
  146.0 2.2 %slice_add_fusion.1 = (f32[4,48,768]{2,1,0:T(8,128)S(1)}, f32[4,48,768]{2,1,0:T(8,128)}) fusion(f32[8,48,768]{2,1,0:T(8,128)} %collective-permute-done.10, f32[8,48,768]{2,1,0:T(8,128)S(1)} %copy-done.5), kind=kLoop, calls=%fused_computation.7 | loop fusion | flops 294912 | bytes 3538944 | tf_op jit(solution)/shard_map/add | solution.py:382
  150.3 8.0 %shard_map.243 = (f32[512,768]{1,0:T(8,128)}, f32[512,768]{1,0:T(8,128)}) custom-call(f32[512,768]{1,0:T(8,128)} %shard_map.242.mine, f32[512,768]{1,0:T(8,128)} %collective-permute-done.3.other, bf16[512,768]{1,0:T(8,128)(2,1)} %bitcast.11, f32[1,768]{1,0:T(1,128)} %broadcast_in_dim.26.b_out, f32[2,768]{1,0:T(2,128)} %gain.9, f32[2,768]{1,0:T(2,128)} %shift.5, ...), custom_call_target="tpu_custom_call" | custom-call | tf_op jit(solution)/shard_map/pallas_call | solution.py:338
  160.3 9.5 %collective-permute-done.7 = f32[4,48,768]{2,1,0:T(8,128)} collective-permute-done((f32[4,48,768]{2,1,0:T(8,128)}, f32[4,48,768]{2,1,0:T(8,128)}, u32[]{:S(2)}, u32[]{:S(2)}) %collective-permute-start.7) | collective-permute-done | bytes 589856 | tf_op jit(solution)/shard_map/ppermute | solution.py:374
  172.4 2.1 %collective-permute-start.8 = (f32[2,48,768]{2,1,0:T(8,128)S(1)}, f32[2,48,768]{2,1,0:T(8,128)S(1)}, u32[]{:S(2)}, u32[]{:S(2)}) collective-permute-start(f32[2,48,768]{2,1,0:T(8,128)S(1)} %get-tuple-element.106), channel_id=1, source_target_pairs={{0,8},{2,10},{4,12},{6,14},{8,0},{10,2},{12,4},{14,6},{16,24},{18,... | collective-permute-start | bytes 884744 | tf_op jit(solution)/shard_map/ppermute | solution.py:374
  177.0 3.7 %collective-permute-done.8 = f32[2,48,768]{2,1,0:T(8,128)S(1)} collective-permute-done((f32[2,48,768]{2,1,0:T(8,128)S(1)}, f32[2,48,768]{2,1,0:T(8,128)S(1)}, u32[]{:S(2)}, u32[]{:S(2)}) %collective-permute-start.8) | collective-permute-done | bytes 294944 | tf_op jit(solution)/shard_map/ppermute | solution.py:374
  182.0 3.0 %collective-permute-done.12 = f32[2,48,768]{2,1,0:T(8,128)S(1)} collective-permute-done((f32[2,48,768]{2,1,0:T(8,128)S(1)}, f32[2,48,768]{2,1,0:T(8,128)S(1)}, u32[]{:S(2)}, u32[]{:S(2)}) %collective-permute-start.12) | collective-permute-done | bytes 294944 | tf_op jit(solution)/shard_map/ppermute | solution.py:374
  185.7 2.9 %collective-permute-start.13 = (f32[1,48,768]{2,1,0:T(8,128)S(1)}, f32[1,48,768]{2,1,0:T(8,128)S(1)}, u32[]{:S(2)}, u32[]{:S(2)}) collective-permute-start(f32[1,48,768]{2,1,0:T(8,128)S(1)} %get-tuple-element.107), channel_id=1, source_target_pairs={{0,16},{2,18},{4,20},{6,22},{8,24},{10,26},{12,28},{14,30},{16,0},... | collective-permute-start | bytes 442376 | tf_op jit(solution)/shard_map/ppermute | solution.py:374
  194.5 3.0 %collective-permute-done.13.got_b = f32[1,48,768]{2,1,0:T(8,128)S(1)} collective-permute-done((f32[1,48,768]{2,1,0:T(8,128)S(1)}, f32[1,48,768]{2,1,0:T(8,128)S(1)}, u32[]{:S(2)}, u32[]{:S(2)}) %collective-permute-start.13) | collective-permute-done | bytes 147488 | tf_op jit(solution)/shard_map/ppermute | solution.py:374
  200.0 3.9 %shard_map.244 = bf16[512,768]{1,0:T(8,128)(2,1)} custom-call(f32[512,768]{1,0:T(8,128)} %get-tuple-element.71.mine, f32[512,768]{1,0:T(8,128)} %collective-permute-done.4.other, f32[512,768]{1,0:T(8,128)} %get-tuple-element.72.h_one, f32[1,768]{1,0:T(1,128)} %broadcast_in_dim.28.b_back, f32[2,768]{1,0:T(2,128)} %gain.9, f32[2,768]{1,0:T(2,128)} %shift.5), custom_call_target="tpu_custom_call" | custom-call | tf_op jit(solution)/shard_map/pallas_call | solution.py:338
  (104 shorter events, 46.3 us)
Async XLA Ops:
  25.9 14.8 %collective-permute-start.20 = (f32[128,768]{1,0:T(8,128)}, f32[128,768]{1,0:T(8,128)S(1)}, u32[]{:S(2)}, u32[]{:S(2)}) collective-permute-start(f32[128,768]{1,0:T(8,128)} %get-tuple-element.83), channel_id=1, source_target_pairs={{0,24},{2,26},{4,28},{6,30},{8,0},{10,2},{12,4},{14,6},{16,8},{18,... | collective-permute-start | bytes 1179656 | tf_op jit(solution)/shard_map/ppermute | solution.py:412
  30.9 19.1 %collective-permute-start.19 = (f32[128,768]{1,0:T(8,128)}, f32[128,768]{1,0:T(8,128)S(1)}, u32[]{:S(2)}, u32[]{:S(2)}) collective-permute-start(f32[128,768]{1,0:T(8,128)} %get-tuple-element.83), channel_id=1, source_target_pairs={{0,8},{2,10},{4,12},{6,14},{8,16},{10,18},{12,20},{14,22},{16,24},... | collective-permute-start | bytes 1179656 | tf_op jit(solution)/shard_map/ppermute | solution.py:412
  30.9 34.0 %collective-permute-start.18 = (f32[128,768]{1,0:T(8,128)}, f32[128,768]{1,0:T(8,128)S(1)}, u32[]{:S(2)}, u32[]{:S(2)}) collective-permute-start(f32[128,768]{1,0:T(8,128)} %get-tuple-element.83), channel_id=1, source_target_pairs={{0,16},{2,18},{4,20},{6,22},{8,24},{10,26},{12,28},{14,30},{16,0},... | collective-permute-start | bytes 1179656 | tf_op jit(solution)/shard_map/ppermute | solution.py:412
  31.9 34.9 %collective-permute-start.2 = (f32[128,768]{1,0:T(8,128)}, f32[128,768]{1,0:T(8,128)S(1)}, u32[]{:S(2)}, u32[]{:S(2)}) collective-permute-start(f32[128,768]{1,0:T(8,128)} %get-tuple-element.57.mine), channel_id=1, source_target_pairs={{0,1},{1,0},{2,3},{3,2},{4,5},{5,4},{6,7},{7,6},{8,9},{9,8},{10,11... | collective-permute-start | bytes 1179656 | tf_op jit(solution)/shard_map/ppermute | solution.py:371
  66.1 62.2 %collective-permute-start.21 = (f32[384,768]{1,0:T(8,128)}, f32[384,768]{1,0:T(8,128)S(1)}, u32[]{:S(2)}, u32[]{:S(2)}) collective-permute-start(f32[384,768]{1,0:T(8,128)} %pad_maximum_fusion), channel_id=1, source_target_pairs={{0,1},{1,0},{2,3},{3,2},{4,5},{5,4},{6,7},{7,6},{8,9},{9,8},{10,11... | collective-permute-start | bytes 3538952 | tf_op jit(solution)/shard_map/ppermute | solution.py:371
  78.1 63.3 %collective-permute-start.6 = (f32[8,48,768]{2,1,0:T(8,128)}, f32[8,48,768]{2,1,0:T(8,128)}, u32[]{:S(2)}, u32[]{:S(2)}) collective-permute-start(f32[8,48,768]{2,1,0:T(8,128)} %get-tuple-element.77), channel_id=1, source_target_pairs={{0,2},{2,0},{4,6},{6,4},{8,10},{10,8},{12,14},{14,12},{16,18},{18,... | collective-permute-start | bytes 3538952 | tf_op jit(solution)/shard_map/ppermute | solution.py:374
  85.4 62.9 %collective-permute-start.3 = (f32[512,768]{1,0:T(8,128)}, f32[512,768]{1,0:T(8,128)}, u32[]{:S(2)}, u32[]{:S(2)}) collective-permute-start(f32[512,768]{1,0:T(8,128)} %shard_map.242.mine), channel_id=1, source_target_pairs={{0,1},{1,0},{2,3},{3,2},{4,5},{5,4},{6,7},{7,6},{8,9},{9,8},{10,11... | collective-permute-start | bytes 4718600 | tf_op jit(solution)/shard_map/ppermute | solution.py:371
  85.6 22.2 %collective-permute-start.14 = (f32[8,1536]{1,0:T(8,128)S(1)}, f32[8,1536]{1,0:T(8,128)S(1)}, u32[]{:S(2)}, u32[]{:S(2)}) collective-permute-start(f32[8,1536]{1,0:T(8,128)S(1)} %copy-done.14), channel_id=1, source_target_pairs={{0,2},{2,0},{4,6},{6,4},{8,10},{10,8},{12,14},{14,12},{16,18},{18,... | collective-permute-start | bytes 147464 | tf_op jit(solution)/shard_map/ppermute | solution.py:374
  86.1 59.4 %collective-permute-start.10 = (f32[8,48,768]{2,1,0:T(8,128)}, f32[8,48,768]{2,1,0:T(8,128)}, u32[]{:S(2)}, u32[]{:S(2)}) collective-permute-start(f32[8,48,768]{2,1,0:T(8,128)} %get-tuple-element.79), channel_id=1, source_target_pairs={{0,4},{2,6},{4,0},{6,2},{8,12},{10,14},{12,8},{14,10},{16,20},{18,... | collective-permute-start | bytes 3538952 | tf_op jit(solution)/shard_map/ppermute | solution.py:374
  107.8 7.5 %collective-permute-start.15 = (f32[8,1536]{1,0:T(8,128)S(1)}, f32[8,1536]{1,0:T(8,128)S(1)}, u32[]{:S(2)}, u32[]{:S(2)}) collective-permute-start(f32[8,1536]{1,0:T(8,128)S(1)} %add.222), channel_id=1, source_target_pairs={{0,4},{2,6},{4,0},{6,2},{8,12},{10,14},{12,8},{14,10},{16,20},{18,... | collective-permute-start | bytes 147464 | tf_op jit(solution)/shard_map/ppermute | solution.py:374
  115.2 4.2 %collective-permute-start.16 = (f32[8,1536]{1,0:T(8,128)S(1)}, f32[8,1536]{1,0:T(8,128)S(1)}, u32[]{:S(2)}, u32[]{:S(2)}) collective-permute-start(f32[8,1536]{1,0:T(8,128)S(1)} %add.223), channel_id=1, source_target_pairs={{0,8},{2,10},{4,12},{6,14},{8,0},{10,2},{12,4},{14,6},{16,24},{18,... | collective-permute-start | bytes 147464 | tf_op jit(solution)/shard_map/ppermute | solution.py:374
  119.4 7.6 %collective-permute-start.17 = (f32[8,1536]{1,0:T(8,128)S(1)}, f32[8,1536]{1,0:T(8,128)S(1)}, u32[]{:S(2)}, u32[]{:S(2)}) collective-permute-start(f32[8,1536]{1,0:T(8,128)S(1)} %add.224), channel_id=1, source_target_pairs={{0,16},{2,18},{4,20},{6,22},{8,24},{10,26},{12,28},{14,30},{16,0},... | collective-permute-start | bytes 147464 | tf_op jit(solution)/shard_map/ppermute | solution.py:374
  127.0 58.7 %collective-permute-start.5 = (f32[512,768]{1,0:T(8,128)}, f32[512,768]{1,0:T(8,128)S(1)}, u32[]{:S(2)}, u32[]{:S(2)}) collective-permute-start(f32[512,768]{1,0:T(8,128)} %shard_map.245), channel_id=1, source_target_pairs={{0,1},{1,0},{2,3},{3,2},{4,5},{5,4},{6,7},{7,6},{8,9},{9,8},{10,11... | collective-permute-start | bytes 4718600 | tf_op jit(solution)/shard_map/ppermute | solution.py:371
  138.0 20.2 %collective-permute-start.22 = (f32[2,48,1536]{2,1,0:T(8,128)}, f32[2,48,1536]{2,1,0:T(8,128)}, u32[]{:S(2)}, u32[]{:S(2)}) collective-permute-start(f32[2,48,1536]{2,1,0:T(8,128)} %get-tuple-element.85), channel_id=1, source_target_pairs={{0,2},{2,0},{4,6},{6,4},{8,10},{10,8},{12,14},{14,12},{16,18},{18,... | collective-permute-start | bytes 1769480 | tf_op jit(solution)/shard_map/ppermute | solution.py:374
  141.3 34.3 %collective-permute-start.24 = (f32[2,48,1536]{2,1,0:T(8,128)}, f32[2,48,1536]{2,1,0:T(8,128)S(1)}, u32[]{:S(2)}, u32[]{:S(2)}) collective-permute-start(f32[2,48,1536]{2,1,0:T(8,128)} %get-tuple-element.87), channel_id=1, source_target_pairs={{0,4},{2,6},{4,0},{6,2},{8,12},{10,14},{12,8},{14,10},{16,20},{18,... | collective-permute-start | bytes 1769480 | tf_op jit(solution)/shard_map/ppermute | solution.py:374
  145.5 24.2 %collective-permute-start.7 = (f32[4,48,768]{2,1,0:T(8,128)}, f32[4,48,768]{2,1,0:T(8,128)}, u32[]{:S(2)}, u32[]{:S(2)}) collective-permute-start(f32[4,48,768]{2,1,0:T(8,128)} %get-tuple-element.98), channel_id=1, source_target_pairs={{0,4},{2,6},{4,0},{6,2},{8,12},{10,14},{12,8},{14,10},{16,20},{18,... | collective-permute-start | bytes 1769480 | tf_op jit(solution)/shard_map/ppermute | solution.py:374
  148.2 24.2 %collective-permute-start.11 = (f32[4,48,768]{2,1,0:T(8,128)}, f32[4,48,768]{2,1,0:T(8,128)}, u32[]{:S(2)}, u32[]{:S(2)}) collective-permute-start(f32[4,48,768]{2,1,0:T(8,128)} %get-tuple-element.96), channel_id=1, source_target_pairs={{0,8},{2,10},{4,12},{6,14},{8,0},{10,2},{12,4},{14,6},{16,24},{18,... | collective-permute-start | bytes 1769480 | tf_op jit(solution)/shard_map/ppermute | solution.py:374
  158.2 41.7 %collective-permute-start.4 = (f32[512,768]{1,0:T(8,128)}, f32[512,768]{1,0:T(8,128)}, u32[]{:S(2)}, u32[]{:S(2)}) collective-permute-start(f32[512,768]{1,0:T(8,128)} %get-tuple-element.71.mine), channel_id=1, source_target_pairs={{0,1},{1,0},{2,3},{3,2},{4,5},{5,4},{6,7},{7,6},{8,9},{9,8},{10,11... | collective-permute-start | bytes 4718600 | tf_op jit(solution)/shard_map/ppermute | solution.py:371
  169.8 20.2 %collective-permute-start.23 = (f32[1,48,1536]{2,1,0:T(8,128)S(1)}, f32[1,48,1536]{2,1,0:T(8,128)S(1)}, u32[]{:S(2)}, u32[]{:S(2)}) collective-permute-start(f32[1,48,1536]{2,1,0:T(8,128)S(1)} %get-tuple-element.101), channel_id=1, source_target_pairs={{0,4},{2,6},{4,0},{6,2},{8,12},{10,14},{12,8},{14,10},{16,20},{18,... | collective-permute-start | bytes 884744 | tf_op jit(solution)/shard_map/ppermute | solution.py:374
  172.4 8.3 %collective-permute-start.8 = (f32[2,48,768]{2,1,0:T(8,128)S(1)}, f32[2,48,768]{2,1,0:T(8,128)S(1)}, u32[]{:S(2)}, u32[]{:S(2)}) collective-permute-start(f32[2,48,768]{2,1,0:T(8,128)S(1)} %get-tuple-element.106), channel_id=1, source_target_pairs={{0,8},{2,10},{4,12},{6,14},{8,0},{10,2},{12,4},{14,6},{16,24},{18,... | collective-permute-start | bytes 884744 | tf_op jit(solution)/shard_map/ppermute | solution.py:374
  175.6 9.3 %collective-permute-start.12 = (f32[2,48,768]{2,1,0:T(8,128)S(1)}, f32[2,48,768]{2,1,0:T(8,128)S(1)}, u32[]{:S(2)}, u32[]{:S(2)}) collective-permute-start(f32[2,48,768]{2,1,0:T(8,128)S(1)} %get-tuple-element.104), channel_id=1, source_target_pairs={{0,2},{2,0},{4,6},{6,4},{8,10},{10,8},{12,14},{14,12},{16,18},{18,... | collective-permute-start | bytes 884744 | tf_op jit(solution)/shard_map/ppermute | solution.py:374
  180.7 9.2 %collective-permute-start.25 = (f32[1,48,1536]{2,1,0:T(8,128)S(1)}, f32[1,48,1536]{2,1,0:T(8,128)S(1)}, u32[]{:S(2)}, u32[]{:S(2)}) collective-permute-start(f32[1,48,1536]{2,1,0:T(8,128)S(1)} %get-tuple-element.99), channel_id=1, source_target_pairs={{0,2},{2,0},{4,6},{6,4},{8,10},{10,8},{12,14},{14,12},{16,18},{18,... | collective-permute-start | bytes 884744 | tf_op jit(solution)/shard_map/ppermute | solution.py:374
  185.0 9.5 %collective-permute-start.9 = (f32[1,48,768]{2,1,0:T(8,128)S(1)}, f32[1,48,768]{2,1,0:T(8,128)S(1)}, u32[]{:S(2)}, u32[]{:S(2)}) collective-permute-start(f32[1,48,768]{2,1,0:T(8,128)S(1)} %get-tuple-element.109), channel_id=1, source_target_pairs={{0,16},{2,18},{4,20},{6,22},{8,24},{10,26},{12,28},{14,30},{16,0},... | collective-permute-start | bytes 442376 | tf_op jit(solution)/shard_map/ppermute | solution.py:374
  185.7 11.8 %collective-permute-start.13 = (f32[1,48,768]{2,1,0:T(8,128)S(1)}, f32[1,48,768]{2,1,0:T(8,128)S(1)}, u32[]{:S(2)}, u32[]{:S(2)}) collective-permute-start(f32[1,48,768]{2,1,0:T(8,128)S(1)} %get-tuple-element.107), channel_id=1, source_target_pairs={{0,16},{2,18},{4,20},{6,22},{8,24},{10,26},{12,28},{14,30},{16,0},... | collective-permute-start | bytes 442376 | tf_op jit(solution)/shard_map/ppermute | solution.py:374
  (20 other events, 101.5 us)
where the time goes:
time: 204 us
  waiting for transfers between devices  83.8 us (41%)
  Pallas kernels  64.5 us (32%)
  starting transfers between devices  26.9 us (13%)
  other arithmetic  16.3 us (8%)
  local copies, waits for them, and re-layouts  11.6 us (6%)
    pallas_call x11, Pallas kernels, call(): return result(*args)  64.5 us
    ppermute x16, waiting for transfers between devices, across(): return lax.ppermute(value, 'dp', [(i, i ^ 1 << bit) for i in range(count)])  49.4 us
    ppermute x3, waiting for transfers between devices, gather_far(): lax.ppermute(value, 'dp', [(i, (i + step * near) % count) for i in range(...  33 us
    ppermute x16, starting transfers between devices, across(): return lax.ppermute(value, 'dp', [(i, i ^ 1 << bit) for i in range(count)])  19.7 us
    add x4, other arithmetic, halve(): keep = keep[:half] + got[:half]  7.08 us
    ppermute x3, starting transfers between devices, gather_far(): lax.ppermute(value, 'dp', [(i, (i + step * near) % count) for i in range(...  5.96 us
    unnamed x36, local copies, waits for them, and re-layouts  5.39 us
    add x4, other arithmetic, halve(): send = keep[half:] + got[half:]  4.18 us
  transfers between devices with their start and end apart: 26, of which 13 were waited for; matrix products, arithmetic and copies ran while one was open for 10% of the time, Pallas kernels for 21%

commit v1 on v0

--- a/solution.py
+++ b/solution.py
@@ -312,17 +312,14 @@
         back_send[c] = d_back[(near + c) * chunk : (near + c + 1) * chunk]
 
 
-def finish_feed_kernel(keep_in, got_in, keep_back, got_back, in_o, back_o):
-    in_o[...] = keep_in[0] + got_in[0]
-    back_o[...] = keep_back[0] + got_back[0]
-
-
-def finish_heads_kernel(keep_a, got_a, keep_b, got_b, out_o, qkv_o):
+def finish_kernel(keep_a, got_a, keep_b, got_b, keep_in, got_in, keep_back, got_back, out_o, qkv_o, in_o, back_o):
     local = out_o.shape[1]
     out_o[...] = keep_a[0, :, :local] + got_a[0, :, :local]
     qkv_o[0] = keep_a[0, :, local:] + got_a[0, :, local:]
     qkv_o[1] = keep_b[0, :, :local] + got_b[0, :, :local]
     qkv_o[2] = keep_b[0, :, local:] + got_b[0, :, local:]
+    in_o[...] = keep_in[0] + got_in[0]
+    back_o[...] = keep_back[0] + got_back[0]
 
 
 def call(kernel, outs, *args, scalars=0, scratch=()):
@@ -391,7 +388,7 @@
     z_low, z_high = bits - 2, bits - 1
     rest = list(range(2, near_bits))
     order_a = [0, 1] + rest + [z_low, z_high]
-    order_b = [1, z_low, 0] + rest + [z_high]
+    order_b = [1, 0] + rest + [z_low, z_high]
     order_in = [0, 1] + rest
     order_back = [1, 0] + rest
     delta = jnp.arange(count, dtype=jnp.int32) ^ me.astype(jnp.int32)
@@ -496,17 +493,20 @@
         last_kernel, [((length, width), LOW)], part, flip(part), h_full, b_back, ln_gain, ln_bias
     )
     grad_tokens = jnp.add(back_part, flip(back_part))
-    for bit in range(bits):
+    for bit in range(bits - 1):
         small = small + across(small, bit)
+    small_got = across(small, bits - 1)
     last_a = halve(a_keep, a_send, order_a)
     last_b = halve(b_keep, b_send, order_b)
     last_in = halve(in_keep, in_send, order_in)
     last_back = halve(back_keep, back_send, order_back)
-    sum_in, sum_back = call(
-        finish_feed_kernel, [((chunk, hidden), F32)] * 2, *last_in, *last_back
-    )
-    sum_out, sum_qkv = call(
-        finish_heads_kernel, [((chunk, local), F32), ((3, chunk, local), F32)], *last_a, *last_b
+    small, keep_in, keep_back = lax.optimization_barrier((small, last_in[0], last_back[0]))
+    small = small + small_got
+    last_in, last_back = (keep_in, last_in[1]), (keep_back, last_back[1])
+    sum_out, sum_qkv, sum_in, sum_back = call(
+        finish_kernel,
+        [((chunk, local), F32), ((3, chunk, local), F32), ((chunk, hidden), F32), ((chunk, hidden), F32)],
+        *last_a, *last_b, *last_in, *last_back,
     )
     return (
         output[None],

time: 204 us -> 201 us (0.985)
    pallas_call x11 -> x10, Pallas kernels: 64.5 us -> 62.9 us  [call(): return result(*args)]
    unnamed x36 -> x40, local copies, waits for them, and re-layouts: 5.39 us -> 4.08 us
  transfers between devices with their start and end apart: 26 -> 26, of which waited for: 13 -> 12; matrix products, arithmetic and copies ran while one was open for 10% -> 11% of each run, Pallas kernels for 21% -> 20%
where the time goes in v1:
time: 201 us
  waiting for transfers between devices  84.1 us (42%)
  Pallas kernels  62.9 us (31%)
  starting transfers between devices  25.3 us (13%)
  other arithmetic  17.1 us (9%)
  local copies, waits for them, and re-layouts  10.3 us (5%)
    pallas_call x10, Pallas kernels, call(): return result(*args)  62.9 us
    ppermute x16, waiting for transfers between devices, across(): return lax.ppermute(value, 'dp', [(i, i ^ 1 << bit) for i in range(count)])  50.3 us
    ppermute x3, waiting for transfers between devices, gather_far(): lax.ppermute(value, 'dp', [(i, (i + step * near) % count) for i in range(...  32.4 us
    ppermute x16, starting transfers between devices, across(): return lax.ppermute(value, 'dp', [(i, i ^ 1 << bit) for i in range(count)])  18.4 us
    add x4, other arithmetic, halve(): keep = keep[:half] + got[:half]  6.86 us
    ppermute x3, starting transfers between devices, gather_far(): lax.ppermute(value, 'dp', [(i, (i + step * near) % count) for i in range(...  5.96 us
    add x4, other arithmetic, halve(): send = keep[half:] + got[half:]  5.31 us
    unnamed x40, local copies, waits for them, and re-layouts  4.08 us
  transfers between devices with their start and end apart: 26, of which 12 were waited for; matrix products, arithmetic and copies ran while one was open for 11% of the time, Pallas kernels for 20%

profile of v1, /device:TPU:0, one launch (start us, length us, event | category | flops | bytes accessed | tf_op | source)
XLA Modules:
  0.0 200.5 jit_solution(5218481858350427438)
XLA Ops:
  2.0 7.7 %shard_map.238 = (bf16[512,384]{1,0:T(8,128)(2,1)}, bf16[512,384]{1,0:T(8,128)(2,1)}, bf16[512,384]{1,0:T(8,128)(2,1)}, bf16[128,384]{1,0:T(8,128)(2,1)}, bf16[1...) custom-call(bf16[512,768]{1,0:T(8,128)(2,1)} %bitcast.9, ...), custom_call_target="tpu_custom_call" | custom-call | tf_op jit(solution)/shard_map/pallas_call | solution.py:335
  12.5 4.8 %shard_map.239 = (f32[128,768]{1,0:T(8,128)}, f32[128,768]{1,0:T(8,128)}, f32[128,768]{1,0:T(8,128)}, f32[128,1]{1,0:T(8,128)}, f32[128,1536]{1,0:T(8,128)}) custom-call(f32[128,768]{1,0:T(8,128)} %get-tuple-element.55.mine, f32[128,768]{1,0:T(8,128)} %copy-done.11, bf16[128,768]{1,0:T(8,128)(2,1)} %get-tuple-element.56.tok.tok_sel, ...), custom_call_target="tpu_custom_call" | custom-call | tf_op jit(solution)/shard_map/pallas_call | solution.py:335
  20.0 5.9 %shard_map.240 = (f32[128,768]{1,0:T(8,128)}, f32[128,768]{1,0:T(8,128)}, f32[128,768]{1,0:T(8,128)}, f32[8,1536]{1,0:T(8,128)}) custom-call(s32[1]{0:T(128)} %bitcast.2.mpi, f32[128,768]{1,0:T(8,128)} %get-tuple-element.57.mine, f32[128,768]{1,0:T(8,128)} %copy-done.10, f32[128,768]{1,0:T(8,128)} %get-tuple-element.58.h_one, ...), custom_call_target="tpu_custom_call" | custom-call | tf_op jit(solution)/shard_map/pallas_call | solution.py:335
  25.9 4.9 %collective-permute-start.19 = (f32[128,768]{1,0:T(8,128)}, f32[128,768]{1,0:T(8,128)S(1)}, u32[]{:S(2)}, u32[]{:S(2)}) collective-permute-start(f32[128,768]{1,0:T(8,128)} %get-tuple-element.84), channel_id=1, source_target_pairs={{0,24},{2,26},{4,28},{6,30},{8,0},{10,2},{12,4},{14,6},{16,8},{18,... | collective-permute-start | bytes 1179656 | tf_op jit(solution)/shard_map/ppermute | solution.py:409
  32.4 8.3 %collective-permute-done.19.far_c = f32[128,768]{1,0:T(8,128)S(1)} collective-permute-done((f32[128,768]{1,0:T(8,128)}, f32[128,768]{1,0:T(8,128)S(1)}, u32[]{:S(2)}, u32[]{:S(2)}) %collective-permute-start.19) | collective-permute-done | bytes 393248 | tf_op jit(solution)/shard_map/ppermute | solution.py:409
  40.7 9.3 %collective-permute-done.18.far_b = f32[128,768]{1,0:T(8,128)S(1)} collective-permute-done((f32[128,768]{1,0:T(8,128)}, f32[128,768]{1,0:T(8,128)S(1)}, u32[]{:S(2)}, u32[]{:S(2)}) %collective-permute-start.18) | collective-permute-done | bytes 393248 | tf_op jit(solution)/shard_map/ppermute | solution.py:409
  50.0 14.9 %collective-permute-done.17.far_a = f32[128,768]{1,0:T(8,128)S(1)} collective-permute-done((f32[128,768]{1,0:T(8,128)}, f32[128,768]{1,0:T(8,128)S(1)}, u32[]{:S(2)}, u32[]{:S(2)}) %collective-permute-start.17) | collective-permute-done | bytes 393248 | tf_op jit(solution)/shard_map/ppermute | solution.py:409
  66.9 10.4 %shard_map.241 = (f32[8,48,768]{2,1,0:T(8,128)}, f32[8,48,768]{2,1,0:T(8,128)}, f32[8,48,768]{2,1,0:T(8,128)}, f32[8,48,768]{2,1,0:T(8,128)}, bf16[128,384]{1,0:...) custom-call(s32[2,16]{1,0:T(2,128)} %pad_add_fusion.place, ...), custom_call_target="tpu_custom_call" | custom-call | tf_op jit(solution)/shard_map/pallas_call | solution.py:335
  78.8 5.5 %shard_map.245 = f32[512,768]{1,0:T(8,128)} custom-call(s32[1]{0:T(128)} %bitcast.2.mpi, bf16[128,384]{1,0:T(8,128)(2,1)} %get-tuple-element.76.g_q, bf16[512,384]{1,0:T(8,128)(2,1)} %get-tuple-element.77.g_k, bf16[512,384]{1,0:T(8,128)(2,1)} %get-tuple-element.78.g_v, bf16[3,768,384]{2,1,0:T(8,128)(2,1)} %w_qkv.3, s32[128,1]{1,0:T(8,128)} %copy.27.pos, ...), custom_call_target="tpu_custom_call" | custom-call | tf_op jit(solution)/shard_map/pallas_call | solution.py:335
  86.4 20.6 %collective-permute-done.14 = f32[8,1536]{1,0:T(8,128)S(1)} collective-permute-done((f32[8,1536]{1,0:T(8,128)S(1)}, f32[8,1536]{1,0:T(8,128)S(1)}, u32[]{:S(2)}, u32[]{:S(2)}) %collective-permute-start.14) | collective-permute-done | bytes 49184 | tf_op jit(solution)/shard_map/ppermute | solution.py:371
  108.6 5.4 %collective-permute-done.15 = f32[8,1536]{1,0:T(8,128)S(1)} collective-permute-done((f32[8,1536]{1,0:T(8,128)S(1)}, f32[8,1536]{1,0:T(8,128)S(1)}, u32[]{:S(2)}, u32[]{:S(2)}) %collective-permute-start.15) | collective-permute-done | bytes 49184 | tf_op jit(solution)/shard_map/ppermute | solution.py:371
  114.1 5.7 %shard_map.242.mine = f32[512,768]{1,0:T(8,128)} custom-call(bf16[512,384]{1,0:T(8,128)(2,1)} %get-tuple-element.73.query, bf16[512,384]{1,0:T(8,128)(2,1)} %get-tuple-element.66.keys, bf16[512,384]{1,0:T(8,128)(2,1)} %get-tuple-element.67.values, bf16[384,768]{1,0:T(8,128)(2,1)} %w_out.5), custom_call_target="tpu_custom_call" | custom-call | tf_op jit(solution)/shard_map/pallas_call | solution.py:335
  121.7 3.3 %collective-permute-start.25 = (f32[8,1536]{1,0:T(8,128)S(1)}, f32[8,1536]{1,0:T(8,128)S(1)}, u32[]{:S(2)}, u32[]{:S(2)}) collective-permute-start(f32[8,1536]{1,0:T(8,128)S(1)} %add.224), channel_id=1, source_target_pairs={{0,16},{2,18},{4,20},{6,22},{8,24},{10,26},{12,28},{14,30},{16,0},... | collective-permute-start | bytes 147464 | tf_op jit(solution)/shard_map/ppermute | solution.py:371
  125.0 8.6 %shard_map.246 = (f32[2,48,1536]{2,1,0:T(8,128)}, f32[2,48,1536]{2,1,0:T(8,128)}, f32[2,48,1536]{2,1,0:T(8,128)}, f32[2,48,1536]{2,1,0:T(8,128)}) custom-call(f32[128,768]{1,0:T(8,128)} %get-tuple-element.58.h_one, f32[128,768]{1,0:T(8,128)} %get-tuple-element.61.grad_z, f32[128,768]{1,0:T(8,128)} %copy-done.3, f32[128,768]{1,0:T(8,128)} %copy-done.2, ...), custom_call_target="tpu_custom_call" | custom-call | tf_op jit(solution)/shard_map/pallas_call | solution.py:335
  134.1 2.3 %slice_add_fusion.3 = (f32[4,48,768]{2,1,0:T(8,128)S(1)}, f32[4,48,768]{2,1,0:T(8,128)}) fusion(f32[8,48,768]{2,1,0:T(8,128)} %collective-permute-done.6, f32[8,48,768]{2,1,0:T(8,128)S(1)} %copy-done.6), kind=kLoop, calls=%fused_computation.9 | loop fusion | flops 294912 | bytes 3538944 | tf_op jit(solution)/shard_map/add | solution.py:379
  137.9 2.3 %slice_add_fusion.1 = (f32[4,48,768]{2,1,0:T(8,128)S(1)}, f32[4,48,768]{2,1,0:T(8,128)}) fusion(f32[8,48,768]{2,1,0:T(8,128)} %collective-permute-done.10, f32[8,48,768]{2,1,0:T(8,128)S(1)} %copy-done.5), kind=kLoop, calls=%fused_computation.7 | loop fusion | flops 294912 | bytes 3538944 | tf_op jit(solution)/shard_map/add | solution.py:379
  143.6 7.9 %shard_map.243 = (f32[512,768]{1,0:T(8,128)}, f32[512,768]{1,0:T(8,128)}) custom-call(f32[512,768]{1,0:T(8,128)} %shard_map.242.mine, f32[512,768]{1,0:T(8,128)} %collective-permute-done.3.other, bf16[512,768]{1,0:T(8,128)(2,1)} %bitcast.11, f32[1,768]{1,0:T(1,128)} %broadcast_in_dim.26.b_out, f32[2,768]{1,0:T(2,128)} %gain.9, f32[2,768]{1,0:T(2,128)} %shift.5, ...), custom_call_target="tpu_custom_call" | custom-call | tf_op jit(solution)/shard_map/pallas_call | solution.py:335
  157.1 8.4 %collective-permute-done.7 = f32[4,48,768]{2,1,0:T(8,128)} collective-permute-done((f32[4,48,768]{2,1,0:T(8,128)}, f32[4,48,768]{2,1,0:T(8,128)}, u32[]{:S(2)}, u32[]{:S(2)}) %collective-permute-start.7) | collective-permute-done | bytes 589856 | tf_op jit(solution)/shard_map/ppermute | solution.py:371
  169.4 2.1 %collective-permute-start.12 = (f32[2,48,768]{2,1,0:T(8,128)S(1)}, f32[2,48,768]{2,1,0:T(8,128)S(1)}, u32[]{:S(2)}, u32[]{:S(2)}) collective-permute-start(f32[2,48,768]{2,1,0:T(8,128)S(1)} %get-tuple-element.110), channel_id=1, source_target_pairs={{0,8},{2,10},{4,12},{6,14},{8,0},{10,2},{12,4},{14,6},{16,24},{18,... | collective-permute-start | bytes 884744 | tf_op jit(solution)/shard_map/ppermute | solution.py:371
  172.1 7.6 %collective-permute-done.8 = f32[2,48,768]{2,1,0:T(8,128)S(1)} collective-permute-done((f32[2,48,768]{2,1,0:T(8,128)S(1)}, f32[2,48,768]{2,1,0:T(8,128)S(1)}, u32[]{:S(2)}, u32[]{:S(2)}) %collective-permute-start.8) | collective-permute-done | bytes 294944 | tf_op jit(solution)/shard_map/ppermute | solution.py:371
  180.4 2.5 %collective-permute-done.12 = f32[2,48,768]{2,1,0:T(8,128)S(1)} collective-permute-done((f32[2,48,768]{2,1,0:T(8,128)S(1)}, f32[2,48,768]{2,1,0:T(8,128)S(1)}, u32[]{:S(2)}, u32[]{:S(2)}) %collective-permute-start.12) | collective-permute-done | bytes 294944 | tf_op jit(solution)/shard_map/ppermute | solution.py:371
  186.6 4.2 %collective-permute-done.9.got_a = f32[1,48,768]{2,1,0:T(8,128)S(1)} collective-permute-done((f32[1,48,768]{2,1,0:T(8,128)S(1)}, f32[1,48,768]{2,1,0:T(8,128)S(1)}, u32[]{:S(2)}, u32[]{:S(2)}) %collective-permute-start.9) | collective-permute-done | bytes 147488 | tf_op jit(solution)/shard_map/ppermute | solution.py:371
  193.1 2.4 %shard_map.247 = (f32[48,384]{1,0:T(8,128)}, f32[3,48,384]{2,1,0:T(8,128)}, f32[48,1536]{1,0:T(8,128)}, f32[48,1536]{1,0:T(8,128)}) custom-call(f32[1,48,768]{2,1,0:T(8,128)} %get-tuple-element.116.keep_a, f32[1,48,768]{2,1,0:T(8,128)} %copy-done.14, f32[1,48,768]{2,1,0:T(8,128)} %get-tuple-element.114.keep_b, f32[1,48,768]{2,1,0:T(8,128)} %copy-done.15, ...), custom_call_target="tpu_custom_call" | custom-call | tf_op jit(solution)/shard_map/pallas_call | solution.py:335
  196.7 3.9 %shard_map.244 = bf16[512,768]{1,0:T(8,128)(2,1)} custom-call(f32[512,768]{1,0:T(8,128)} %get-tuple-element.74.mine, f32[512,768]{1,0:T(8,128)} %copy-done.4, f32[512,768]{1,0:T(8,128)} %get-tuple-element.75.h_one, f32[1,768]{1,0:T(1,128)} %broadcast_in_dim.28.b_back, f32[2,768]{1,0:T(2,128)} %gain.9, f32[2,768]{1,0:T(2,128)} %shift.5), custom_call_target="tpu_custom_call" | custom-call | tf_op jit(solution)/shard_map/pallas_call | solution.py:335
  (107 shorter events, 40.9 us)
Async XLA Ops:
  25.9 14.8 %collective-permute-start.19 = (f32[128,768]{1,0:T(8,128)}, f32[128,768]{1,0:T(8,128)S(1)}, u32[]{:S(2)}, u32[]{:S(2)}) collective-permute-start(f32[128,768]{1,0:T(8,128)} %get-tuple-element.84), channel_id=1, source_target_pairs={{0,24},{2,26},{4,28},{6,30},{8,0},{10,2},{12,4},{14,6},{16,8},{18,... | collective-permute-start | bytes 1179656 | tf_op jit(solution)/shard_map/ppermute | solution.py:409
  30.8 19.1 %collective-permute-start.18 = (f32[128,768]{1,0:T(8,128)}, f32[128,768]{1,0:T(8,128)S(1)}, u32[]{:S(2)}, u32[]{:S(2)}) collective-permute-start(f32[128,768]{1,0:T(8,128)} %get-tuple-element.84), channel_id=1, source_target_pairs={{0,8},{2,10},{4,12},{6,14},{8,16},{10,18},{12,20},{14,22},{16,24},... | collective-permute-start | bytes 1179656 | tf_op jit(solution)/shard_map/ppermute | solution.py:409
  30.8 34.0 %collective-permute-start.17 = (f32[128,768]{1,0:T(8,128)}, f32[128,768]{1,0:T(8,128)S(1)}, u32[]{:S(2)}, u32[]{:S(2)}) collective-permute-start(f32[128,768]{1,0:T(8,128)} %get-tuple-element.84), channel_id=1, source_target_pairs={{0,16},{2,18},{4,20},{6,22},{8,24},{10,26},{12,28},{14,30},{16,0},... | collective-permute-start | bytes 1179656 | tf_op jit(solution)/shard_map/ppermute | solution.py:409
  31.8 34.3 %collective-permute-start.2 = (f32[128,768]{1,0:T(8,128)}, f32[128,768]{1,0:T(8,128)S(1)}, u32[]{:S(2)}, u32[]{:S(2)}) collective-permute-start(f32[128,768]{1,0:T(8,128)} %get-tuple-element.60.mine), channel_id=1, source_target_pairs={{0,1},{1,0},{2,3},{3,2},{4,5},{5,4},{6,7},{7,6},{8,9},{9,8},{10,11... | collective-permute-start | bytes 1179656 | tf_op jit(solution)/shard_map/ppermute | solution.py:368
  66.0 55.7 %collective-permute-start.20 = (f32[384,768]{1,0:T(8,128)}, f32[384,768]{1,0:T(8,128)}, u32[]{:S(2)}, u32[]{:S(2)}) collective-permute-start(f32[384,768]{1,0:T(8,128)} %pad_maximum_fusion), channel_id=1, source_target_pairs={{0,1},{1,0},{2,3},{3,2},{4,5},{5,4},{6,7},{7,6},{8,9},{9,8},{10,11... | collective-permute-start | bytes 3538952 | tf_op jit(solution)/shard_map/ppermute | solution.py:368
  77.3 56.3 %collective-permute-start.6 = (f32[8,48,768]{2,1,0:T(8,128)}, f32[8,48,768]{2,1,0:T(8,128)}, u32[]{:S(2)}, u32[]{:S(2)}) collective-permute-start(f32[8,48,768]{2,1,0:T(8,128)} %get-tuple-element.80), channel_id=1, source_target_pairs={{0,2},{2,0},{4,6},{6,4},{8,10},{10,8},{12,14},{14,12},{16,18},{18,... | collective-permute-start | bytes 3538952 | tf_op jit(solution)/shard_map/ppermute | solution.py:371
  84.4 55.9 %collective-permute-start.5 = (f32[512,768]{1,0:T(8,128)}, f32[512,768]{1,0:T(8,128)S(1)}, u32[]{:S(2)}, u32[]{:S(2)}) collective-permute-start(f32[512,768]{1,0:T(8,128)} %shard_map.245), channel_id=1, source_target_pairs={{0,1},{1,0},{2,3},{3,2},{4,5},{5,4},{6,7},{7,6},{8,9},{9,8},{10,11... | collective-permute-start | bytes 4718600 | tf_op jit(solution)/shard_map/ppermute | solution.py:368
  84.4 52.1 %collective-permute-start.10 = (f32[8,48,768]{2,1,0:T(8,128)}, f32[8,48,768]{2,1,0:T(8,128)}, u32[]{:S(2)}, u32[]{:S(2)}) collective-permute-start(f32[8,48,768]{2,1,0:T(8,128)} %get-tuple-element.82), channel_id=1, source_target_pairs={{0,4},{2,6},{4,0},{6,2},{8,12},{10,14},{12,8},{14,10},{16,20},{18,... | collective-permute-start | bytes 3538952 | tf_op jit(solution)/shard_map/ppermute | solution.py:371
  85.9 21.1 %collective-permute-start.14 = (f32[8,1536]{1,0:T(8,128)S(1)}, f32[8,1536]{1,0:T(8,128)S(1)}, u32[]{:S(2)}, u32[]{:S(2)}) collective-permute-start(f32[8,1536]{1,0:T(8,128)S(1)} %copy-done.16), channel_id=1, source_target_pairs={{0,2},{2,0},{4,6},{6,4},{8,10},{10,8},{12,14},{14,12},{16,18},{18,... | collective-permute-start | bytes 147464 | tf_op jit(solution)/shard_map/ppermute | solution.py:371
  107.0 7.0 %collective-permute-start.15 = (f32[8,1536]{1,0:T(8,128)S(1)}, f32[8,1536]{1,0:T(8,128)S(1)}, u32[]{:S(2)}, u32[]{:S(2)}) collective-permute-start(f32[8,1536]{1,0:T(8,128)S(1)} %add.222), channel_id=1, source_target_pairs={{0,4},{2,6},{4,0},{6,2},{8,12},{10,14},{12,8},{14,10},{16,20},{18,... | collective-permute-start | bytes 147464 | tf_op jit(solution)/shard_map/ppermute | solution.py:371
  114.0 5.8 %collective-permute-start.16 = (f32[8,1536]{1,0:T(8,128)S(1)}, f32[8,1536]{1,0:T(8,128)S(1)}, u32[]{:S(2)}, u32[]{:S(2)}) collective-permute-start(f32[8,1536]{1,0:T(8,128)S(1)} %add.223), channel_id=1, source_target_pairs={{0,8},{2,10},{4,12},{6,14},{8,0},{10,2},{12,4},{14,6},{16,24},{18,... | collective-permute-start | bytes 147464 | tf_op jit(solution)/shard_map/ppermute | solution.py:371
  119.8 22.3 %collective-permute-start.3 = (f32[512,768]{1,0:T(8,128)}, f32[512,768]{1,0:T(8,128)}, u32[]{:S(2)}, u32[]{:S(2)}) collective-permute-start(f32[512,768]{1,0:T(8,128)} %shard_map.242.mine), channel_id=1, source_target_pairs={{0,1},{1,0},{2,3},{3,2},{4,5},{5,4},{6,7},{7,6},{8,9},{9,8},{10,11... | collective-permute-start | bytes 4718600 | tf_op jit(solution)/shard_map/ppermute | solution.py:368
  121.7 47.7 %collective-permute-start.25 = (f32[8,1536]{1,0:T(8,128)S(1)}, f32[8,1536]{1,0:T(8,128)S(1)}, u32[]{:S(2)}, u32[]{:S(2)}) collective-permute-start(f32[8,1536]{1,0:T(8,128)S(1)} %add.224), channel_id=1, source_target_pairs={{0,16},{2,18},{4,20},{6,22},{8,24},{10,26},{12,28},{14,30},{16,0},... | collective-permute-start | bytes 147464 | tf_op jit(solution)/shard_map/ppermute | solution.py:371
  133.6 18.0 %collective-permute-start.21 = (f32[2,48,1536]{2,1,0:T(8,128)}, f32[2,48,1536]{2,1,0:T(8,128)}, u32[]{:S(2)}, u32[]{:S(2)}) collective-permute-start(f32[2,48,1536]{2,1,0:T(8,128)} %get-tuple-element.86), channel_id=1, source_target_pairs={{0,2},{2,0},{4,6},{6,4},{8,10},{10,8},{12,14},{14,12},{16,18},{18,... | collective-permute-start | bytes 1769480 | tf_op jit(solution)/shard_map/ppermute | solution.py:371
  136.4 17.3 %collective-permute-start.22 = (f32[2,48,1536]{2,1,0:T(8,128)}, f32[2,48,1536]{2,1,0:T(8,128)}, u32[]{:S(2)}, u32[]{:S(2)}) collective-permute-start(f32[2,48,1536]{2,1,0:T(8,128)} %get-tuple-element.88), channel_id=1, source_target_pairs={{0,4},{2,6},{4,0},{6,2},{8,12},{10,14},{12,8},{14,10},{16,20},{18,... | collective-permute-start | bytes 1769480 | tf_op jit(solution)/shard_map/ppermute | solution.py:371
  140.3 25.3 %collective-permute-start.7 = (f32[4,48,768]{2,1,0:T(8,128)}, f32[4,48,768]{2,1,0:T(8,128)}, u32[]{:S(2)}, u32[]{:S(2)}) collective-permute-start(f32[4,48,768]{2,1,0:T(8,128)} %get-tuple-element.104), channel_id=1, source_target_pairs={{0,4},{2,6},{4,0},{6,2},{8,12},{10,14},{12,8},{14,10},{16,20},{18,... | collective-permute-start | bytes 1769480 | tf_op jit(solution)/shard_map/ppermute | solution.py:371
  142.1 26.0 %collective-permute-start.11 = (f32[4,48,768]{2,1,0:T(8,128)}, f32[4,48,768]{2,1,0:T(8,128)}, u32[]{:S(2)}, u32[]{:S(2)}) collective-permute-start(f32[4,48,768]{2,1,0:T(8,128)} %get-tuple-element.102), channel_id=1, source_target_pairs={{0,2},{2,0},{4,6},{6,4},{8,10},{10,8},{12,14},{14,12},{16,18},{18,... | collective-permute-start | bytes 1769480 | tf_op jit(solution)/shard_map/ppermute | solution.py:371
  151.6 43.9 %collective-permute-start.4 = (f32[512,768]{1,0:T(8,128)}, f32[512,768]{1,0:T(8,128)S(1)}, u32[]{:S(2)}, u32[]{:S(2)}) collective-permute-start(f32[512,768]{1,0:T(8,128)} %get-tuple-element.74.mine), channel_id=1, source_target_pairs={{0,1},{1,0},{2,3},{3,2},{4,5},{5,4},{6,7},{7,6},{8,9},{9,8},{10,11... | collective-permute-start | bytes 4718600 | tf_op jit(solution)/shard_map/ppermute | solution.py:368
  153.7 32.9 %collective-permute-start.23 = (f32[1,48,1536]{2,1,0:T(8,128)}, f32[1,48,1536]{2,1,0:T(8,128)S(1)}, u32[]{:S(2)}, u32[]{:S(2)}) collective-permute-start(f32[1,48,1536]{2,1,0:T(8,128)} %get-tuple-element.107), channel_id=1, source_target_pairs={{0,4},{2,6},{4,0},{6,2},{8,12},{10,14},{12,8},{14,10},{16,20},{18,... | collective-permute-start | bytes 884744 | tf_op jit(solution)/shard_map/ppermute | solution.py:371
  165.6 21.0 %collective-permute-start.24 = (f32[1,48,1536]{2,1,0:T(8,128)}, f32[1,48,1536]{2,1,0:T(8,128)S(1)}, u32[]{:S(2)}, u32[]{:S(2)}) collective-permute-start(f32[1,48,1536]{2,1,0:T(8,128)} %get-tuple-element.105), channel_id=1, source_target_pairs={{0,2},{2,0},{4,6},{6,4},{8,10},{10,8},{12,14},{14,12},{16,18},{18,... | collective-permute-start | bytes 884744 | tf_op jit(solution)/shard_map/ppermute | solution.py:371
  168.2 11.5 %collective-permute-start.8 = (f32[2,48,768]{2,1,0:T(8,128)S(1)}, f32[2,48,768]{2,1,0:T(8,128)S(1)}, u32[]{:S(2)}, u32[]{:S(2)}) collective-permute-start(f32[2,48,768]{2,1,0:T(8,128)S(1)} %get-tuple-element.112), channel_id=1, source_target_pairs={{0,8},{2,10},{4,12},{6,14},{8,0},{10,2},{12,4},{14,6},{16,24},{18,... | collective-permute-start | bytes 884744 | tf_op jit(solution)/shard_map/ppermute | solution.py:371
  169.4 13.4 %collective-permute-start.12 = (f32[2,48,768]{2,1,0:T(8,128)S(1)}, f32[2,48,768]{2,1,0:T(8,128)S(1)}, u32[]{:S(2)}, u32[]{:S(2)}) collective-permute-start(f32[2,48,768]{2,1,0:T(8,128)S(1)} %get-tuple-element.110), channel_id=1, source_target_pairs={{0,8},{2,10},{4,12},{6,14},{8,0},{10,2},{12,4},{14,6},{16,24},{18,... | collective-permute-start | bytes 884744 | tf_op jit(solution)/shard_map/ppermute | solution.py:371
  180.4 10.4 %collective-permute-start.9 = (f32[1,48,768]{2,1,0:T(8,128)S(1)}, f32[1,48,768]{2,1,0:T(8,128)S(1)}, u32[]{:S(2)}, u32[]{:S(2)}) collective-permute-start(f32[1,48,768]{2,1,0:T(8,128)S(1)} %get-tuple-element.115), channel_id=1, source_target_pairs={{0,16},{2,18},{4,20},{6,22},{8,24},{10,26},{12,28},{14,30},{16,0},... | collective-permute-start | bytes 442376 | tf_op jit(solution)/shard_map/ppermute | solution.py:371
  183.5 8.9 %collective-permute-start.13 = (f32[1,48,768]{2,1,0:T(8,128)S(1)}, f32[1,48,768]{2,1,0:T(8,128)S(1)}, u32[]{:S(2)}, u32[]{:S(2)}) collective-permute-start(f32[1,48,768]{2,1,0:T(8,128)S(1)} %get-tuple-element.113), channel_id=1, source_target_pairs={{0,16},{2,18},{4,20},{6,22},{8,24},{10,26},{12,28},{14,30},{16,0},... | collective-permute-start | bytes 442376 | tf_op jit(solution)/shard_map/ppermute | solution.py:371
  (22 other events, 125.1 us)
